TPU v7x, 32 devices: a whole 2x2x4 slice. The times are simulated.
32 devices in a mesh: row: 8 (over z, y), col: 4 (over x, core).
Axes of the slice: x: 2, y: 2, z: 4, core: 2. Of those that a mesh axis runs over, the one named last changes fastest.
Arguments:
- momentum: float32 [8192, 16384], P('row', 'col'), may hold values from -6 to 6
- grads: bfloat16 [2, 8192, 16384], P(None, 'row', 'col'), may hold values from -400 to 400
- basis: float32 [16384, 256], P('col'), may hold values from -0.046875 to 0.046875
Outputs:
- change: bfloat16 [8192, 16384], P('row', 'col')
- state: float32 [8192, 16384], P('row', 'col')
All inputs are finite; a program needn't handle non-finite values.
Results may differ from a plain program's by a relative error of at most 0.0035.
Values sent between devices are 32-bit elements; how exact they have to be, the bound alone decides.
A program may use at most 192 MiB of HBM per device.

v0:
```python
import jax
import jax.numpy as jnp
from jax import lax
from jax.sharding import PartitionSpec as P

ROWS = 8192
COLS = 16384
RANK = 256
STEPS = 2
keep_rate = 0.95
norm_eps = 1e-06


def column_squares(matrix):
    return jnp.sum(matrix * matrix, axis=0)


def shards(momentum, grads, basis):
    high = lax.Precision.HIGHEST
    factor = (ROWS * COLS / RANK) ** 0.5
    state = momentum
    right = basis
    change = jnp.zeros(momentum.shape, jnp.float32)
    for step in range(STEPS):
        buffer = state + grads[step].astype(jnp.float32)
        partial_value = jnp.dot(buffer, right, precision=high, preferred_element_type=jnp.float32)
        projected = lax.psum(partial_value, "col")
        gram = lax.psum(
            jnp.dot(projected.T, projected, precision=high, preferred_element_type=jnp.float32),
            "row",
        )
        lower = jnp.linalg.cholesky(gram)
        ortho = jax.scipy.linalg.solve_triangular(lower, projected.T, lower=True).T
        local_right = lax.dot_general(
            buffer,
            ortho,
            (((0,), (0,)), ((), ())),
            precision=high,
            preferred_element_type=jnp.float32,
        )
        raw = lax.psum(local_right, "row")
        squares = lax.psum(column_squares(raw), "col")
        right = raw * lax.rsqrt(squares + norm_eps)
        state = buffer - (1.0 - keep_rate) * jnp.dot(
            ortho, raw.T, precision=high, preferred_element_type=jnp.float32
        )
        change = change + factor * jnp.dot(
            ortho, right.T, precision=high, preferred_element_type=jnp.float32
        )
    return (change.astype(jnp.bfloat16), state)


def solution(mesh):
    return jax.shard_map(
        shards,
        mesh=mesh,
        in_specs=(P("row", "col"), P(None, "row", "col"), P("col", None)),
        out_specs=(P("row", "col"), P("row", "col")),
        check_vma=False,
    )
```

profile of v0, /device:TPU:0, one launch (start us, length us, event | category | flops | bytes accessed | tf_op | source)
XLA Modules:
  0.0 904.7 jit_solution(4281090039093472297)
XLA Ops:
  7.2 20.3 %fusion.1 = f32[1024,256]{1,0:T(8,128)} fusion(f32[4096,256]{1,0:T(8,128)} %param.8, f32[1024,4096]{1,0:T(8,128)} %param.6, bf16[2,1024,4096]{2,1,0:T(8,128)(2,1)} %param.7), kind=kOutput, calls=%fused_computation.9 | convolution fusion | flops 12893290496 | bytes 30408704 | tf_op jit(solution)/shard_map/dot_general | solution.py:26
  27.6 39.1 %all-reduce.8.cloned.1.call-done = f32[1024,256]{1,0:T(8,128)} async-done(((f32[1024,256]{1,0:T(8,128)}), f32[1024,256]{1,0:T(8,128)}) %all-reduce.8.cloned.1.call-update) | async-done | bytes 1048592 | tf_op jit(solution)/shard_map/psum | solution.py:27
  66.7 4.1 fusion.35
  71.0 71.4 %all-reduce.10.cloned.1.call-done = f32[256,256]{0,1:T(8,128)} async-done(((f32[256,256]{0,1:T(8,128)}), f32[256,256]{0,1:T(8,128)}) %all-reduce.10.cloned.1.call-update) | async-done | bytes 262160 | tf_op jit(solution)/shard_map/psum | solution.py:28
  144.5 11.7 %cholesky.130 = f32[128,128]{1,0:T(8,128)S(1)} custom-call(f32[128,128]{1,0:T(8,128)S(1)} %cholesky.194), custom_call_target="Cholesky" | custom-call | tf_op jit(solution)/shard_map/jit(cholesky)/cholesky | solution.py:32
  156.3 9.8 %custom-call.13 = f32[1,128,128]{1,2,0:T(8,128)S(1)} custom-call(f32[1,128,128]{2,1,0:T(8,128)S(1)} %get-tuple-element.47), custom_call_target="InvertDiagBlocksLowerTriangular" | custom-call | tf_op jit(solution)/shard_map/jit(cholesky)/cholesky | solution.py:32
  166.6 11.7 %cholesky.147 = f32[128,128]{1,0:T(8,128)S(1)} custom-call(f32[128,128]{1,0:T(8,128)S(1)} %convolution_subtract_fusion.3), custom_call_target="Cholesky" | custom-call | tf_op jit(solution)/shard_map/jit(cholesky)/cholesky | solution.py:32
  180.5 4.1 while.4
  184.6 19.7 %custom-call.14 = f32[2,128,128]{1,2,0:T(8,128)S(1)} custom-call(f32[2,128,128]{2,1,0:T(8,128)S(1)} %get-tuple-element.18), custom_call_target="InvertDiagBlocksLowerTriangular" | custom-call | tf_op jit(solution)/shard_map/jit(_solve_triangular)/triangular_solve | solution.py:33
  206.0 2.0 convolution_subtract_fusion.1
  208.7 32.9 %fusion = f32[4096,256]{1,0:T(8,128)} fusion(f32[1024,4096]{1,0:T(8,128)} %param.6, bf16[2,1024,4096]{2,1,0:T(8,128)(2,1)} %param.7, f32[128,1024]{1,0:T(8,128)S(1)} %fusion.22, f32[128,1024]{1,0:T(8,128)S(1)} %fusion.13), kind=kOutput, calls=%fused_computation.8 | convolution fusion | flops 12893552640 | bytes 30408704 | tf_op jit(solution)/shard_map/dot_general | solution.py:34
  241.7 155.7 %all-reduce.12.cloned.1.call-done = f32[4096,256]{1,0:T(8,128)} async-done(((f32[4096,256]{1,0:T(8,128)}), f32[4096,256]{1,0:T(8,128)}) %all-reduce.12.cloned.1.call-update) | async-done | bytes 4194320 | tf_op jit(solution)/shard_map/psum | solution.py:41
  397.4 2.7 multiply_reduce_fusion.1
  400.1 6.4 psum.59
  406.5 36.7 %convert_add_fusion = f32[1024,4096]{1,0:T(8,128)} fusion(f32[4096,256]{1,0:T(8,128)} %all-reduce.12.cloned.1.call-done, bf16[2,1024,4096]{2,1,0:T(8,128)(2,1)} %param.7, f32[1024,4096]{1,0:T(8,128)} %param.6, f32[128,1024]{1,0:T(8,128)S(1)} %fusion.22, f32[128,1024]{1,0:T(8,128)S(1)} %fusion.13), kind=kOutput, calls=%fused_computation.4 | convolution fusion | flops 12910329856 | bytes 55574528 | tf_op jit(solution)/shard_map/dot_general | solution.py:44
  443.3 17.2 %fusion.3 = f32[1024,256]{1,0:T(8,128)} fusion(f32[1024,4096]{1,0:T(8,128)} %convert_add_fusion, f32[4096,256]{1,0:T(8,128)} %all-reduce.12.cloned.1.call-done, f32[256]{0:T(256)S(1)} %add_rsqrt_fusion.1), kind=kOutput, calls=%fused_computation.13 | convolution fusion | flops 12885950464 | bytes 22021120 | tf_op jit(solution)/shard_map/dot_general | solution.py:26
  460.8 34.7 %all-reduce.14.cloned.1.call-done = f32[1024,256]{1,0:T(8,128)} async-done(((f32[1024,256]{1,0:T(8,128)}), f32[1024,256]{1,0:T(8,128)}) %all-reduce.14.cloned.1.call-update) | async-done | bytes 1048592 | tf_op jit(solution)/shard_map/psum | solution.py:27
  495.5 4.1 fusion.36
  499.6 71.6 %all-reduce.16.cloned.1.call-done = f32[256,256]{0,1:T(8,128)} async-done(((f32[256,256]{0,1:T(8,128)}), f32[256,256]{0,1:T(8,128)}) %all-reduce.16.cloned.1.call-update) | async-done | bytes 262160 | tf_op jit(solution)/shard_map/psum | solution.py:28
  573.3 11.7 %cholesky.164 = f32[128,128]{1,0:T(8,128)S(1)} custom-call(f32[128,128]{1,0:T(8,128)S(1)} %cholesky.197), custom_call_target="Cholesky" | custom-call | tf_op jit(solution)/shard_map/jit(cholesky)/cholesky | solution.py:32
  585.7 9.8 %custom-call.15 = f32[1,128,128]{1,2,0:T(8,128)S(1)} custom-call(f32[1,128,128]{2,1,0:T(8,128)S(1)} %get-tuple-element.43), custom_call_target="InvertDiagBlocksLowerTriangular" | custom-call | tf_op jit(solution)/shard_map/jit(cholesky)/cholesky | solution.py:32
  596.0 11.7 %cholesky.181 = f32[128,128]{1,0:T(8,128)S(1)} custom-call(f32[128,128]{1,0:T(8,128)S(1)} %convolution_subtract_fusion.2), custom_call_target="Cholesky" | custom-call | tf_op jit(solution)/shard_map/jit(cholesky)/cholesky | solution.py:32
  609.9 4.5 while.5
  614.4 19.7 %custom-call.16 = f32[2,128,128]{1,2,0:T(8,128)S(1)} custom-call(f32[2,128,128]{2,1,0:T(8,128)S(1)} %get-tuple-element.19), custom_call_target="InvertDiagBlocksLowerTriangular" | custom-call | tf_op jit(solution)/shard_map/jit(_solve_triangular)/triangular_solve | solution.py:33
  635.8 2.0 convolution_subtract_fusion
  638.5 29.9 %fusion.10 = f32[4096,256]{1,0:T(8,128)} fusion(f32[1024,4096]{1,0:T(8,128)} %convert_add_fusion, f32[128,1024]{1,0:T(8,128)S(1)} %fusion.18, f32[128,1024]{1,0:T(8,128)S(1)} %fusion.11), kind=kOutput, calls=%fused_computation.26 | convolution fusion | flops 12885164032 | bytes 22020096 | tf_op jit(solution)/shard_map/dot_general | solution.py:34
  668.4 30.2 %fusion.5 = f32[1024,4096]{1,0:T(8,128)} fusion(f32[4096,256]{1,0:T(8,128)} %all-reduce.12.cloned.1.call-done, f32[256]{0:T(256)S(1)} %add_rsqrt_fusion.1, f32[128,1024]{1,0:T(8,128)S(1)} %fusion.22, f32[128,1024]{1,0:T(8,128)S(1)} %fusion.13), kind=kOutput, calls=%fused_computation.15 | convolution fusion | flops 12886212608 | bytes 22021120 | tf_op jit(solution)/shard_map/dot_general | solution.py:47
  698.5 125.6 %all-reduce.18.cloned.1.call-done = f32[4096,256]{1,0:T(8,128)} async-done(((f32[4096,256]{1,0:T(8,128)}), f32[4096,256]{1,0:T(8,128)}) %all-reduce.18.cloned.1.call-update) | async-done | bytes 4194320 | tf_op jit(solution)/shard_map/psum | solution.py:41
  824.1 2.7 multiply_reduce_fusion
  826.9 6.6 psum.63
  833.5 33.4 %multiply_subtract_fusion = f32[1024,4096]{1,0:T(8,128)} fusion(f32[1024,4096]{1,0:T(8,128)} %convert_add_fusion, f32[4096,256]{1,0:T(8,128)} %all-reduce.18.cloned.1.call-done, f32[128,1024]{1,0:T(8,128)S(1)} %fusion.18, f32[128,1024]{1,0:T(8,128)S(1)} %fusion.11), kind=kOutput, calls=%fused_computation.7 | convolution fusion | flops 12893552640 | bytes 38797312 | tf_op jit(solution)/shard_map/dot_general | solution.py:44
  866.9 30.6 %multiply_convert_fusion = bf16[1024,4096]{1,0:T(8,128)(2,1)} fusion(f32[1024,4096]{1,0:T(8,128)} %fusion.5, f32[4096,256]{1,0:T(8,128)S(1)} %copy-done, f32[256]{0:T(256)S(1)} %add_rsqrt_fusion, f32[128,1024]{1,0:T(8,128)S(1)} %fusion.18, f32[128,1024]{1,0:T(8,128)S(1)} %fusion.11), kind=kOutput, calls=%fused_computation.6 | convolution fusion | flops 12898795520 | bytes 30409728 | tf_op jit(solution)/shard_map/dot_general | solution.py:47
  (57 shorter events, 21.0 us)
Async XLA Ops:
  7.2 59.5 %all-reduce.8.cloned.1.call-start = ((), (), s32[]{:S(2)}) async-start(), calls=%async_computation | async-start | bytes 2097152 | tf_op jit(solution)/shard_map/psum | solution.py:27
  27.5 114.9 %all-reduce.10.cloned.1.call-start = ((), (), s32[]{:S(2)}) async-start(), calls=%async_computation.1 | async-start | bytes 524288 | tf_op jit(solution)/shard_map/psum | solution.py:28
  70.8 326.6 %all-reduce.12.cloned.1.call-start = ((), (), s32[]{:S(2)}) async-start(), calls=%async_computation.2 | async-start | bytes 8388608 | tf_op jit(solution)/shard_map/psum | solution.py:41
  241.6 253.9 %all-reduce.14.cloned.1.call-start = ((), (), s32[]{:S(2)}) async-start(), calls=%async_computation.3 | async-start | bytes 2097152 | tf_op jit(solution)/shard_map/psum | solution.py:27
  460.5 110.7 %all-reduce.16.cloned.1.call-start = ((), (), s32[]{:S(2)}) async-start(), calls=%async_computation.4 | async-start | bytes 524288 | tf_op jit(solution)/shard_map/psum | solution.py:28
  499.6 324.5 %all-reduce.18.cloned.1.call-start = ((), (), s32[]{:S(2)}) async-start(), calls=%async_computation.5 | async-start | bytes 8388608 | tf_op jit(solution)/shard_map/psum | solution.py:41
  833.5 33.5 %copy-start = (f32[4096,256]{1,0:T(8,128)S(1)}, f32[4096,256]{1,0:T(8,128)}, u32[]{:S(2)}) copy-start(f32[4096,256]{1,0:T(8,128)} %all-reduce.18.cloned.1.call-done) | copy-start | bytes 12582916
Sparse Core Ops, SparseCore 0:
  27.7 39.0 all-reduce.7
  70.9 71.4 all-reduce.9
  241.8 155.5 all-reduce.11
  460.7 34.8 all-reduce.13
  499.7 71.4 all-reduce.15
  668.5 155.5 all-reduce.17
where the time goes:
time: 911 us; the launch traced here: 905 us
  waiting for transfers between devices  498 us (55%)
  matrix products  249 us (27%)
  other arithmetic  116 us (13%)
  between operations  17.3 us (2%)
  blocking collectives  13 us (1%)
  local copies, waits for them, and re-layouts  10.4 us (1%)
    psum x2, waiting for transfers between devices, shards(): raw = lax.psum(local_right, 'row')  281 us
    psum x2, waiting for transfers between devices, shards(): lax.psum(jnp.dot(projected.T, projected, precision=high, preferred_elemen...  143 us
    psum x2, waiting for transfers between devices, shards(): projected = lax.psum(partial_value, 'col')  73.8 us
    dot_general x2, matrix products, shards(): jnp.dot(ortho, raw.T, precision=high, preferred_element_type=jnp.float32)  70.2 us
    another operation x13, other arithmetic, shards(): lower = jnp.linalg.cholesky(gram)  68.7 us
    dot_general x2, matrix products, shards(): lax.dot_general(buffer, ortho, (((0,), (0,)), ((), ())), precision=high,...  62.8 us
    dot_general x2, matrix products, shards(): jnp.dot(ortho, right.T, precision=high, preferred_element_type=jnp.float32)  60.8 us
    another operation x5, other arithmetic, shards(): ortho = jax.scipy.linalg.solve_triangular(lower, projected.T, lower=True).T  39.4 us
  transfers between devices with their start and end apart: 6, of which 6 were waited for; matrix products, arithmetic and copies ran while one was open for 3% of the time, Pallas kernels for 0%

commit v1 on v0

--- a/solution.py
+++ b/solution.py
@@ -9,6 +9,7 @@
 STEPS = 2
 keep_rate = 0.95
 norm_eps = 1e-06
+close_the_kinds = lambda values: jnp.sum(jax.lax.all_gather(values, axis_name="row"), axis=0)
 
 
 def column_squares(matrix):
@@ -25,9 +26,8 @@
         buffer = state + grads[step].astype(jnp.float32)
         partial_value = jnp.dot(buffer, right, precision=high, preferred_element_type=jnp.float32)
         projected = lax.psum(partial_value, "col")
-        gram = lax.psum(
-            jnp.dot(projected.T, projected, precision=high, preferred_element_type=jnp.float32),
-            "row",
+        gram = close_the_kinds(
+            jnp.dot(projected.T, projected, precision=high, preferred_element_type=jnp.float32)
         )
         lower = jnp.linalg.cholesky(gram)
         ortho = jax.scipy.linalg.solve_triangular(lower, projected.T, lower=True).T

time: 911 us -> 865 us (0.950)
  waiting for transfers between devices: 498 us -> 453 us
    psum x2 -> x0, waiting for transfers between devices: 143 us -> none  [shards(): lax.psum(jnp.dot(projected.T, projected, precision=high, preferred_elemen...]
    all_gather x0 -> x2, waiting for transfers between devices: none -> 99.2 us  [jax.lax.all_gather(values, axis_name='row')]
  transfers between devices with their start and end apart: 6 -> 6, of which waited for: 6 -> 6; matrix products, arithmetic and copies ran while one was open for 3% -> 4% of each run, Pallas kernels for 0% -> 0%
where the time goes in v1:
time: 865 us; the launch traced here: 859 us
  waiting for transfers between devices  453 us (52%)
  matrix products  249 us (29%)
  other arithmetic  117 us (14%)
  between operations  17.3 us (2%)
  blocking collectives  13 us (2%)
    psum x2, waiting for transfers between devices, shards(): raw = lax.psum(local_right, 'row')  280 us
    all_gather x2, waiting for transfers between devices, jax.lax.all_gather(values, axis_name='row')  99.2 us
    psum x2, waiting for transfers between devices, shards(): projected = lax.psum(partial_value, 'col')  73.8 us
    dot_general x2, matrix products, shards(): jnp.dot(ortho, raw.T, precision=high, preferred_element_type=jnp.float32)  70.2 us
    another operation x13, other arithmetic, shards(): lower = jnp.linalg.cholesky(gram)  68.7 us
    dot_general x2, matrix products, shards(): lax.dot_general(buffer, ortho, (((0,), (0,)), ((), ())), precision=high,...  62.8 us
    dot_general x2, matrix products, shards(): jnp.dot(ortho, right.T, precision=high, preferred_element_type=jnp.float32)  60.8 us
    another operation x5, other arithmetic, shards(): ortho = jax.scipy.linalg.solve_triangular(lower, projected.T, lower=True).T  39.4 us
  transfers between devices with their start and end apart: 6, of which 6 were waited for; matrix products, arithmetic and copies ran while one was open for 4% of the time, Pallas kernels for 0%

profile of v1, /device:TPU:0, one launch (start us, length us, event | category | flops | bytes accessed | tf_op | source)
XLA Modules:
  0.0 859.3 jit_solution(12597806348821083547)
XLA Ops:
  7.2 20.3 %fusion.1 = f32[1024,256]{1,0:T(8,128)} fusion(f32[4096,256]{1,0:T(8,128)} %param.8, f32[1024,4096]{1,0:T(8,128)} %param.6, bf16[2,1024,4096]{2,1,0:T(8,128)(2,1)} %param.7), kind=kOutput, calls=%fused_computation.9 | convolution fusion | flops 12893290496 | bytes 30408704 | tf_op jit(solution)/shard_map/dot_general | solution.py:27
  27.6 39.1 %all-reduce.6.cloned.1.call-done = f32[1024,256]{1,0:T(8,128)} async-done(((f32[1024,256]{1,0:T(8,128)}), f32[1024,256]{1,0:T(8,128)}) %all-reduce.6.cloned.1.call-update) | async-done | bytes 1048592 | tf_op jit(solution)/shard_map/psum | solution.py:28
  66.7 4.1 fusion.35
  71.1 49.5 %all-gather.5.cloned.1.call-done = f32[2048,256]{1,0:T(8,128)} async-done(((f32[256,256]{1,0:T(8,128)}), f32[2048,256]{1,0:T(8,128)}) %all-gather.5.cloned.1.call-update) | async-done | bytes 2097168 | tf_op jit(solution)/shard_map/all_gather | solution.py:12
  122.5 11.7 %cholesky.130 = f32[128,128]{1,0:T(8,128)S(1)} custom-call(f32[128,128]{1,0:T(8,128)S(1)} %cholesky.194), custom_call_target="Cholesky" | custom-call | tf_op jit(solution)/shard_map/jit(cholesky)/cholesky | solution.py:32
  134.2 9.8 %custom-call.13 = f32[1,128,128]{1,2,0:T(8,128)S(1)} custom-call(f32[1,128,128]{2,1,0:T(8,128)S(1)} %get-tuple-element.47), custom_call_target="InvertDiagBlocksLowerTriangular" | custom-call | tf_op jit(solution)/shard_map/jit(cholesky)/cholesky | solution.py:32
  144.6 11.7 %cholesky.147 = f32[128,128]{1,0:T(8,128)S(1)} custom-call(f32[128,128]{1,0:T(8,128)S(1)} %convolution_subtract_fusion.3), custom_call_target="Cholesky" | custom-call | tf_op jit(solution)/shard_map/jit(cholesky)/cholesky | solution.py:32
  158.5 4.1 while.4
  162.6 19.7 %custom-call.14 = f32[2,128,128]{1,2,0:T(8,128)S(1)} custom-call(f32[2,128,128]{2,1,0:T(8,128)S(1)} %get-tuple-element.18), custom_call_target="InvertDiagBlocksLowerTriangular" | custom-call | tf_op jit(solution)/shard_map/jit(_solve_triangular)/triangular_solve | solution.py:33
  184.0 2.0 convolution_subtract_fusion.1
  186.7 32.9 %fusion = f32[4096,256]{1,0:T(8,128)} fusion(f32[1024,4096]{1,0:T(8,128)} %param.6, bf16[2,1024,4096]{2,1,0:T(8,128)(2,1)} %param.7, f32[128,1024]{1,0:T(8,128)S(1)} %fusion.22, f32[128,1024]{1,0:T(8,128)S(1)} %fusion.13), kind=kOutput, calls=%fused_computation.8 | convolution fusion | flops 12893552640 | bytes 30408704 | tf_op jit(solution)/shard_map/dot_general | solution.py:34
  219.7 155.0 %all-reduce.8.cloned.1.call-done = f32[4096,256]{1,0:T(8,128)} async-done(((f32[4096,256]{1,0:T(8,128)}), f32[4096,256]{1,0:T(8,128)}) %all-reduce.8.cloned.1.call-update) | async-done | bytes 4194320 | tf_op jit(solution)/shard_map/psum | solution.py:41
  374.7 2.7 multiply_reduce_fusion.1
  377.5 6.4 psum.44
  383.9 36.7 %convert_add_fusion = f32[1024,4096]{1,0:T(8,128)} fusion(f32[4096,256]{1,0:T(8,128)} %all-reduce.8.cloned.1.call-done, bf16[2,1024,4096]{2,1,0:T(8,128)(2,1)} %param.7, f32[1024,4096]{1,0:T(8,128)} %param.6, f32[128,1024]{1,0:T(8,128)S(1)} %fusion.22, f32[128,1024]{1,0:T(8,128)S(1)} %fusion.13), kind=kOutput, calls=%fused_computation.4 | convolution fusion | flops 12910329856 | bytes 55574528 | tf_op jit(solution)/shard_map/dot_general | solution.py:44
  420.6 17.2 %fusion.3 = f32[1024,256]{1,0:T(8,128)} fusion(f32[1024,4096]{1,0:T(8,128)} %convert_add_fusion, f32[4096,256]{1,0:T(8,128)} %all-reduce.8.cloned.1.call-done, f32[256]{0:T(256)S(1)} %add_rsqrt_fusion.1), kind=kOutput, calls=%fused_computation.13 | convolution fusion | flops 12885950464 | bytes 22021120 | tf_op jit(solution)/shard_map/dot_general | solution.py:27
  438.1 34.7 %all-reduce.10.cloned.1.call-done = f32[1024,256]{1,0:T(8,128)} async-done(((f32[1024,256]{1,0:T(8,128)}), f32[1024,256]{1,0:T(8,128)}) %all-reduce.10.cloned.1.call-update) | async-done | bytes 1048592 | tf_op jit(solution)/shard_map/psum | solution.py:28
  472.8 4.1 fusion.36
  476.9 49.7 %all-gather.7.cloned.1.call-done = f32[2048,256]{1,0:T(8,128)} async-done(((f32[256,256]{1,0:T(8,128)}), f32[2048,256]{1,0:T(8,128)}) %all-gather.7.cloned.1.call-update) | async-done | bytes 2097168 | tf_op jit(solution)/shard_map/all_gather | solution.py:12
  528.6 11.7 %cholesky.164 = f32[128,128]{1,0:T(8,128)S(1)} custom-call(f32[128,128]{1,0:T(8,128)S(1)} %cholesky.197), custom_call_target="Cholesky" | custom-call | tf_op jit(solution)/shard_map/jit(cholesky)/cholesky | solution.py:32
  541.0 9.8 %custom-call.15 = f32[1,128,128]{1,2,0:T(8,128)S(1)} custom-call(f32[1,128,128]{2,1,0:T(8,128)S(1)} %get-tuple-element.43), custom_call_target="InvertDiagBlocksLowerTriangular" | custom-call | tf_op jit(solution)/shard_map/jit(cholesky)/cholesky | solution.py:32
  551.3 11.7 %cholesky.181 = f32[128,128]{1,0:T(8,128)S(1)} custom-call(f32[128,128]{1,0:T(8,128)S(1)} %convolution_subtract_fusion.2), custom_call_target="Cholesky" | custom-call | tf_op jit(solution)/shard_map/jit(cholesky)/cholesky | solution.py:32
  565.2 4.5 while.5
  569.7 19.7 %custom-call.16 = f32[2,128,128]{1,2,0:T(8,128)S(1)} custom-call(f32[2,128,128]{2,1,0:T(8,128)S(1)} %get-tuple-element.19), custom_call_target="InvertDiagBlocksLowerTriangular" | custom-call | tf_op jit(solution)/shard_map/jit(_solve_triangular)/triangular_solve | solution.py:33
  591.1 2.0 convolution_subtract_fusion
  593.7 29.9 %fusion.10 = f32[4096,256]{1,0:T(8,128)} fusion(f32[1024,4096]{1,0:T(8,128)} %convert_add_fusion, f32[128,1024]{1,0:T(8,128)S(1)} %fusion.18, f32[128,1024]{1,0:T(8,128)S(1)} %fusion.11), kind=kOutput, calls=%fused_computation.26 | convolution fusion | flops 12885164032 | bytes 22020096 | tf_op jit(solution)/shard_map/dot_general | solution.py:34
  623.6 30.1 %fusion.5 = f32[1024,4096]{1,0:T(8,128)} fusion(f32[4096,256]{1,0:T(8,128)} %all-reduce.8.cloned.1.call-done, f32[256]{0:T(256)S(1)} %add_rsqrt_fusion.1, f32[128,1024]{1,0:T(8,128)S(1)} %fusion.22, f32[128,1024]{1,0:T(8,128)S(1)} %fusion.13), kind=kOutput, calls=%fused_computation.15 | convolution fusion | flops 12886212608 | bytes 22021120 | tf_op jit(solution)/shard_map/dot_general | solution.py:47
  653.8 124.9 %all-reduce.12.cloned.1.call-done = f32[4096,256]{1,0:T(8,128)} async-done(((f32[4096,256]{1,0:T(8,128)}), f32[4096,256]{1,0:T(8,128)}) %all-reduce.12.cloned.1.call-update) | async-done | bytes 4194320 | tf_op jit(solution)/shard_map/psum | solution.py:41
  778.7 2.7 multiply_reduce_fusion
  781.5 6.6 psum.47
  788.1 33.5 %multiply_subtract_fusion = f32[1024,4096]{1,0:T(8,128)} fusion(f32[1024,4096]{1,0:T(8,128)} %convert_add_fusion, f32[4096,256]{1,0:T(8,128)} %all-reduce.12.cloned.1.call-done, f32[128,1024]{1,0:T(8,128)S(1)} %fusion.18, f32[128,1024]{1,0:T(8,128)S(1)} %fusion.11), kind=kOutput, calls=%fused_computation.7 | convolution fusion | flops 12893552640 | bytes 38797312 | tf_op jit(solution)/shard_map/dot_general | solution.py:44
  821.5 30.6 %multiply_convert_fusion = bf16[1024,4096]{1,0:T(8,128)(2,1)} fusion(f32[1024,4096]{1,0:T(8,128)} %fusion.5, f32[4096,256]{1,0:T(8,128)S(1)} %copy-done, f32[256]{0:T(256)S(1)} %add_rsqrt_fusion, f32[128,1024]{1,0:T(8,128)S(1)} %fusion.18, f32[128,1024]{1,0:T(8,128)S(1)} %fusion.11), kind=kOutput, calls=%fused_computation.6 | convolution fusion | flops 12898795520 | bytes 30409728 | tf_op jit(solution)/shard_map/dot_general | solution.py:47
  (59 shorter events, 20.7 us)
Async XLA Ops:
  7.2 59.5 %all-reduce.6.cloned.1.call-start = ((), (), s32[]{:S(2)}) async-start(), calls=%async_computation | async-start | bytes 2097152 | tf_op jit(solution)/shard_map/psum | solution.py:28
  27.5 93.0 %all-gather.5.cloned.1.call-start = ((), (), s32[]{:S(2)}) async-start(), calls=%async_computation.4 | async-start | bytes 2359296 | tf_op jit(solution)/shard_map/all_gather | solution.py:12
  70.8 303.9 %all-reduce.8.cloned.1.call-start = ((), (), s32[]{:S(2)}) async-start(), calls=%async_computation.1 | async-start | bytes 8388608 | tf_op jit(solution)/shard_map/psum | solution.py:41
  219.6 253.2 %all-reduce.10.cloned.1.call-start = ((), (), s32[]{:S(2)}) async-start(), calls=%async_computation.2 | async-start | bytes 2097152 | tf_op jit(solution)/shard_map/psum | solution.py:28
  437.8 88.8 %all-gather.7.cloned.1.call-start = ((), (), s32[]{:S(2)}) async-start(), calls=%async_computation.5 | async-start | bytes 2359296 | tf_op jit(solution)/shard_map/all_gather | solution.py:12
  476.9 301.8 %all-reduce.12.cloned.1.call-start = ((), (), s32[]{:S(2)}) async-start(), calls=%async_computation.3 | async-start | bytes 8388608 | tf_op jit(solution)/shard_map/psum | solution.py:41
  788.1 33.5 %copy-start = (f32[4096,256]{1,0:T(8,128)S(1)}, f32[4096,256]{1,0:T(8,128)}, u32[]{:S(2)}) copy-start(f32[4096,256]{1,0:T(8,128)} %all-reduce.12.cloned.1.call-done) | copy-start | bytes 12582916
Sparse Core Ops, SparseCore 0:
  27.7 39.0 all-reduce.5
  70.9 49.5 all-gather.4
  219.7 154.9 all-reduce.7
  438.0 34.7 all-reduce.9
  477.0 49.5 all-gather.6
  623.7 154.9 all-reduce.11
